TPU v7x, 32 devices: a whole 2x2x4 slice. The times are simulated.
32 devices in a mesh: shard: 2 (over x), ctx: 4 (over y, core), tp: 4 (over z).
Axes of the slice: x: 2, y: 2, z: 4, core: 2. Of those that a mesh axis runs over, the one named last changes fastest.
Arguments:
- tokens: bfloat16 [8, 1024, 767], P('shard', 'ctx'), may hold values from -6 to 6
- lengths: int32 [8], P('shard'), may hold values from 256 to 1024, as said below
- first_gain: float32 [768], replicated, may hold values from 0.5 to 1.5
- entry_weight: bfloat16 [3, 768, 768], P(None, ('shard', 'ctx'), 'tp'), may hold values from -0.21875 to 0.21875
- entry_bias: float32 [2, 768], P(None, 'tp'), may hold values from -3 to 3
- exit_weight: bfloat16 [768, 768], P('tp', ('shard', 'ctx')), may hold values from -0.625 to 0.625
- exit_bias: float32 [768], replicated, may hold values from -3 to 3
- second_gain: float32 [768], replicated, may hold values from 0.5 to 1.5
- hidden_weight: bfloat16 [768, 3072], P(('shard', 'ctx'), 'tp'), may hold values from -0.21875 to 0.21875
- hidden_bias: float32 [3072], P('tp'), may hold values from -3 to 3
- return_weight: bfloat16 [3072, 768], P('tp', ('shard', 'ctx')), may hold values from -0.109375 to 0.109375
- return_bias: float32 [768], replicated, may hold values from -3 to 3
- cotangent: bfloat16 [8, 1024, 767], P('shard', 'ctx'), may hold values from -6 to 6
Outputs:
- result: bfloat16 [8, 1024, 767], P('shard', 'ctx')
- tokens_gradient: bfloat16 [8, 1024, 767], P('shard', 'ctx')
- first_gain_gradient: float32 [768], replicated
- entry_weight_gradient: float32 [3, 768, 768], P(None, ('shard', 'ctx'), 'tp')
- entry_bias_gradient: float32 [2, 768], P(None, 'tp')
- exit_weight_gradient: float32 [768, 768], P('tp', ('shard', 'ctx'))
- exit_bias_gradient: float32 [768], replicated
- second_gain_gradient: float32 [768], replicated
- hidden_weight_gradient: float32 [768, 3072], P(('shard', 'ctx'), 'tp')
- hidden_bias_gradient: float32 [3072], P('tp')
- return_weight_gradient: float32 [3072, 768], P('tp', ('shard', 'ctx'))
- return_bias_gradient: float32 [768], replicated
Inputs may be any that keep to these rules, and one draw needn't show every extreme that they name: `lengths`: in every draw some sequence has exactly 1024 valid positions and some has exactly 256.
All inputs are finite; a program needn't handle non-finite values.
Results may differ from a plain program's by a relative error of at most 0.014.
Values may be sent and summed in bfloat16 or wider, within the bound.
No kernel may reach another device: no remote copies, remote signals or barrier semaphores. Data moves between devices by JAX's collectives and lax.ppermute only.
A program may use at most 256 MiB of HBM per device.

v0:
```python
import math
import jax
import jax.numpy as jnp
from jax import lax
from jax.sharding import PartitionSpec as P

HDIM = 64
EPSILON = 1e-05


def row_mean(values):
    return jnp.mean(values, -1, keepdims=True)


def shards(
    tokens,
    lengths,
    first_gain,
    entry_weight,
    entry_bias,
    exit_weight,
    exit_bias,
    second_gain,
    hidden_weight,
    hidden_bias,
    return_weight,
    return_bias,
    cotangent,
):
    seq_dev, local, narrow = tokens.shape
    row_count = seq_dev * local
    full_len = local * lax.axis_size("ctx")
    head_width = entry_weight.shape[2]
    heads_here = head_width // HDIM
    scale = 1.0 / math.sqrt(HDIM)
    bfloat = jnp.bfloat16
    single = jnp.float32
    full_entry, full_exit, full_hidden, full_return = (
        lax.all_gather(entry_weight, ("shard", "ctx"), axis=1, tiled=True),
        lax.all_gather(exit_weight, ("shard", "ctx"), axis=1, tiled=True),
        lax.all_gather(hidden_weight, ("shard", "ctx"), axis=0, tiled=True),
        lax.all_gather(return_weight, ("shard", "ctx"), axis=1, tiled=True),
    )
    stream_part = tokens.astype(single).reshape(row_count, narrow)
    stream = jnp.concatenate([stream_part, -jnp.sum(stream_part, -1, keepdims=True)], 1)
    first_inverse = lax.rsqrt(row_mean(stream * stream) + EPSILON)
    first_unit = stream * first_inverse
    first_normed = (first_unit * first_gain).astype(bfloat)
    queries = (
        jnp.dot(first_normed, full_entry[0], preferred_element_type=single) + entry_bias[0]
    ).astype(bfloat)
    keys = jnp.dot(first_normed, full_entry[1], preferred_element_type=single).astype(bfloat)
    values = (
        jnp.dot(first_normed, full_entry[2], preferred_element_type=single) + entry_bias[1]
    ).astype(bfloat)
    seq_shape = (seq_dev, local, head_width)
    all_keys, all_values = (
        lax.all_gather(keys.reshape(seq_shape), "ctx", axis=1, tiled=True),
        lax.all_gather(values.reshape(seq_shape), "ctx", axis=1, tiled=True),
    )
    offset = lax.axis_index("ctx") * local
    query_pos = offset + jnp.arange(local, dtype=jnp.int32)
    key_pos = jnp.arange(full_len, dtype=jnp.int32)
    local_heads = (seq_dev, local, heads_here, HDIM)
    full_heads = (seq_dev, full_len, heads_here, HDIM)
    allowed = (
        (key_pos[None, None, :] <= query_pos[None, :, None])
        & (key_pos[None, None, :] < lengths[:, None, None])
    )[:, None]

    def masked_scores(query_block, key_block):
        raw_scores = (
            jnp.einsum("sqhd,skhd->shqk", query_block, key_block, preferred_element_type=single)
            * scale
        )
        return jnp.where(allowed, raw_scores, -1e30)

    query_heads = queries.reshape(local_heads)
    scores = masked_scores(query_heads, all_keys.reshape(full_heads))
    largest = jnp.max(scores, -1, keepdims=True)
    exponent = jnp.exp(scores - largest)
    totals = jnp.sum(exponent, -1, keepdims=True)
    weights = (exponent / totals).astype(bfloat)
    log_totals = largest + jnp.log(totals)
    attended = jnp.einsum(
        "shqk,skhd->sqhd", weights, all_values.reshape(full_heads), preferred_element_type=single
    ).astype(bfloat)
    attended_rows = attended.reshape(row_count, head_width)
    exit_term = jnp.dot(attended_rows, full_exit, preferred_element_type=single)
    branch = lax.psum(exit_term, "tp") + exit_bias
    middle = stream + branch - row_mean(branch)
    second_inverse = lax.rsqrt(row_mean(middle * middle) + EPSILON)
    second_unit = middle * second_inverse
    second_normed = (second_unit * second_gain).astype(bfloat)
    hidden = jnp.dot(second_normed, full_hidden, preferred_element_type=single) + hidden_bias
    activated, gelu_pull = jax.vjp(
        lambda values_in: jax.nn.gelu(values_in, approximate=True), hidden
    )
    activated_low = activated.astype(bfloat)
    return_term = jnp.dot(activated_low, full_return, preferred_element_type=single)
    returned = lax.psum(return_term.astype(jnp.bfloat16), "tp").astype(jnp.float32) + return_bias
    full_stream = middle + returned - row_mean(returned)
    result_rows = full_stream[:, :narrow].astype(bfloat)
    result = result_rows.reshape(seq_dev, local, narrow)
    full_entry, full_exit, full_hidden, full_return = (
        lax.all_gather(entry_weight, ("shard", "ctx"), axis=1, tiled=True),
        lax.all_gather(exit_weight, ("shard", "ctx"), axis=1, tiled=True),
        lax.all_gather(hidden_weight, ("shard", "ctx"), axis=0, tiled=True),
        lax.all_gather(return_weight, ("shard", "ctx"), axis=1, tiled=True),
    )
    valid = (query_pos[None, :] < lengths[:, None]).astype(single).reshape(row_count, 1)
    cot_rows = cotangent.astype(single).reshape(row_count, narrow) * valid
    cot_full = jnp.concatenate([cot_rows, jnp.zeros((row_count, 1), single)], 1)
    returned_grad = (cot_full - row_mean(cot_full)).astype(bfloat)
    return_bias_grad = jnp.sum(returned_grad.astype(single), 0)
    return_weight_grad = jnp.einsum(
        "rf,rd->fd", activated_low, returned_grad, preferred_element_type=single
    )
    activated_grad = jnp.einsum(
        "rd,fd->rf", returned_grad, full_return, preferred_element_type=single
    )
    hidden_grad = gelu_pull(activated_grad)[0].astype(bfloat)
    hidden_bias_grad = jnp.sum(hidden_grad.astype(single), 0)
    hidden_weight_grad = jnp.einsum(
        "rd,rf->df", second_normed, hidden_grad, preferred_element_type=single
    )
    second_term = jnp.einsum("rf,df->rd", hidden_grad, full_hidden, preferred_element_type=single)
    second_grad = lax.psum(second_term, "tp")
    second_gain_grad = jnp.sum(second_grad * second_unit, 0)
    second_scaled = second_grad * second_gain
    middle_grad = cot_full + second_inverse * (
        second_scaled - second_unit * row_mean(second_scaled * second_unit)
    )
    branch_grad = (middle_grad - row_mean(middle_grad)).astype(bfloat)
    exit_bias_grad = jnp.sum(branch_grad.astype(single), 0)
    exit_weight_grad = jnp.einsum(
        "re,rd->ed", attended_rows, branch_grad, preferred_element_type=single
    )
    attended_grad = jnp.einsum(
        "rd,ed->re", branch_grad, full_exit, preferred_element_type=single
    ).astype(bfloat)
    all_keys, all_values = (
        lax.all_gather(keys.reshape(seq_shape), "ctx", axis=1, tiled=True),
        lax.all_gather(values.reshape(seq_shape), "ctx", axis=1, tiled=True),
    )
    key_heads = all_keys.reshape(full_heads)
    value_heads = all_values.reshape(full_heads)
    out_grad = attended_grad.reshape(local_heads)
    back_scores = masked_scores(query_heads, key_heads)
    probs = jnp.exp(back_scores - log_totals)
    probs_low = probs.astype(bfloat)
    prob_rounded = lax.optimization_barrier(
        jnp.einsum("sqhd,skhd->shqk", out_grad, value_heads, preferred_element_type=single).astype(
            bfloat
        )
    )
    prob_grad = prob_rounded.astype(single)
    inner = jnp.sum(probs * prob_grad, -1, keepdims=True)
    score_grad = (probs * (prob_grad - inner)).astype(bfloat)
    query_grads = (
        jnp.einsum("shqk,skhd->sqhd", score_grad, key_heads, preferred_element_type=single) * scale
    ).astype(bfloat)
    key_parts = (
        jnp.einsum("shqk,sqhd->skhd", score_grad, query_heads, preferred_element_type=single)
        * scale
    )
    value_parts = jnp.einsum("shqk,sqhd->skhd", probs_low, out_grad, preferred_element_type=single)
    key_sums, value_sums = (
        lax.psum_scatter(
            key_parts.reshape(seq_dev, full_len, head_width), "ctx", scatter_dimension=1, tiled=True
        ),
        lax.psum_scatter(
            value_parts.reshape(seq_dev, full_len, head_width),
            "ctx",
            scatter_dimension=1,
            tiled=True,
        ),
    )
    query_low = query_grads.reshape(row_count, head_width)
    key_low = key_sums.reshape(row_count, head_width).astype(bfloat)
    value_low = value_sums.reshape(row_count, head_width).astype(bfloat)
    entry_bias_grad = jnp.stack(
        [jnp.sum(query_low.astype(single), 0), jnp.sum(value_low.astype(single), 0)]
    )
    entry_weight_grad = jnp.stack(
        [
            jnp.einsum("rd,re->de", first_normed, query_low, preferred_element_type=single),
            jnp.einsum("rd,re->de", first_normed, key_low, preferred_element_type=single),
            jnp.einsum("rd,re->de", first_normed, value_low, preferred_element_type=single),
        ]
    )
    first_part = (
        jnp.einsum("re,de->rd", query_low, full_entry[0], preferred_element_type=single)
        + jnp.einsum("re,de->rd", key_low, full_entry[1], preferred_element_type=single)
        + jnp.einsum("re,de->rd", value_low, full_entry[2], preferred_element_type=single)
    )
    first_grad = lax.psum(first_part, "tp")
    first_gain_grad = jnp.sum(first_grad * first_unit, 0)
    first_scaled = first_grad * first_gain
    stream_grad = middle_grad + first_inverse * (
        first_scaled - first_unit * row_mean(first_scaled * first_unit)
    )
    tokens_rows = (stream_grad[:, :narrow] - stream_grad[:, narrow:]).astype(bfloat)
    tokens_grad = tokens_rows.reshape(seq_dev, local, narrow)
    weight_grads = (
        lax.psum_scatter(entry_weight_grad, ("shard", "ctx"), scatter_dimension=1, tiled=True),
        lax.psum_scatter(exit_weight_grad, ("shard", "ctx"), scatter_dimension=1, tiled=True),
        lax.psum_scatter(hidden_weight_grad, ("shard", "ctx"), scatter_dimension=0, tiled=True),
        lax.psum_scatter(return_weight_grad, ("shard", "ctx"), scatter_dimension=1, tiled=True),
    )
    small_grads = lax.psum(
        (
            first_gain_grad,
            entry_bias_grad,
            exit_bias_grad,
            second_gain_grad,
            hidden_bias_grad,
            return_bias_grad,
        ),
        ("shard", "ctx"),
    )
    return (
        result,
        tokens_grad,
        small_grads[0],
        weight_grads[0],
        small_grads[1],
        weight_grads[1],
        small_grads[2],
        small_grads[3],
        weight_grads[2],
        small_grads[4],
        weight_grads[3],
        small_grads[5],
    )


def solution(mesh):
    return jax.shard_map(
        shards,
        mesh=mesh,
        in_specs=(
            P("shard", "ctx", None),
            P("shard"),
            P(),
            P(None, ("shard", "ctx"), "tp"),
            P(None, "tp"),
            P("tp", ("shard", "ctx")),
            P(),
            P(),
            P(("shard", "ctx"), "tp"),
            P("tp"),
            P("tp", ("shard", "ctx")),
            P(),
            P("shard", "ctx", None),
        ),
        out_specs=(
            P("shard", "ctx", None),
            P("shard", "ctx", None),
            P(),
            P(None, ("shard", "ctx"), "tp"),
            P(None, "tp"),
            P("tp", ("shard", "ctx")),
            P(),
            P(),
            P(("shard", "ctx"), "tp"),
            P("tp"),
            P("tp", ("shard", "ctx")),
            P(),
        ),
        check_vma=False,
    )
```

profile of v0, /device:TPU:0, one launch (start us, length us, event | category | flops | bytes accessed | tf_op | source)
XLA Modules:
  0.0 1059.9 jit_solution(7665863335763462059)
XLA Ops:
  8.1 2.3 convert_reduce_fusion.5
  10.3 2.9 copy.52
  14.5 13.1 %all_gather.24 = bf16[3,768,192]{2,1,0:T(8,128)(2,1)S(1)} all-gather(bf16[3,96,192]{2,1,0:T(8,128)(2,1)S(1)} %copy-done.38), channel_id=1, replica_groups=mesh['shard'=2,'ctx'=4,'tp'=4] {'shard','ctx'}, dimensions={1}, use_global_device_ids=true | all-gather | bytes 995328 | tf_op jit(solution)/shard_map/all_gather | solution.py:39
  36.3 2.9 fusion.21
  42.1 12.4 %all_gather.27 = bf16[192,768]{0,1:T(8,128)(2,1)} all-gather(bf16[192,96]{0,1:T(8,128)(2,1)} %copy.58), channel_id=1, replica_groups=mesh['shard'=2,'ctx'=4,'tp'=4] {'shard','ctx'}, dimensions={1}, use_global_device_ids=true | all-gather | bytes 331776 | tf_op jit(solution)/shard_map/all_gather | solution.py:40
  58.6 2.9 fusion.38
  61.6 4.6 copy-done
  66.2 3.4 fusion.3
  69.6 6.6 all-gather.5.cloned.1.call-done
  78.1 6.6 fusion.24
  85.8 2.2 fusion.39
  89.6 4.3 copy.59
  94.0 2.2 bitcast_multiply_fusion
  99.9 109.4 %all-reduce.7.cloned.1.call-done = f32[1024,768]{1,0:T(8,128)} async-done(((f32[1024,768]{1,0:T(8,128)}), f32[1024,768]{1,0:T(8,128)}) %all-reduce.7.cloned.1.call-update) | async-done | bytes 3145744 | tf_op jit(solution)/shard_map/psum | solution.py:90
  209.3 2.2 add_reduce_fusion
  211.6 4.3 multiply_reduce_fusion.4
  215.9 5.5 fusion.33
  221.4 5.6 convert_reduce_fusion.1
  228.2 3.1 fusion.40
  232.5 119.0 %all-reduce.11.cloned.1.call-done = f32[1024,768]{1,0:T(8,128)} async-done(((f32[1024,768]{1,0:T(8,128)}), f32[1024,768]{1,0:T(8,128)}) %all-reduce.11.cloned.1.call-update) | async-done | bytes 3145744 | tf_op jit(solution)/shard_map/psum | solution.py:128
  351.5 3.5 multiply_reduce_fusion
  363.4 7.6 fusion
  371.1 3.0 fusion.2
  376.7 48.2 %copy.69 = f32[4,1024,192]{0,2,1:T(8,128)} copy(f32[4,1024,192]{1,2,0:T(8,128)S(1)} %bitcast.133) | data formatting | bytes 6291456
  424.9 84.3 %reshape.241 = f32[1024,768]{1,0:T(8,128)} reshape(f32[1024,192,4]{2,1,0:T(8,128)} %bitcast.22) | data formatting | bytes 6291456
  509.8 6.3 fusion.5
  516.1 48.3 %copy.71 = f32[4,1024,192]{0,2,1:T(8,128)} copy(f32[4,1024,192]{1,2,0:T(8,128)S(1)} %bitcast.127) | data formatting | bytes 6291456
  564.3 84.3 %reshape.243 = f32[1024,768]{1,0:T(8,128)} reshape(f32[1024,192,4]{2,1,0:T(8,128)} %bitcast.25) | data formatting | bytes 6291456
  649.9 5.1 convolution_convert_fusion.1
  657.0 5.1 convert_reduce_fusion.4
  663.8 29.2 %reshape.242 = bf16[256,192,4]{2,1,0:T(8,128)(2,1)} reshape(f32[256,768]{1,0:T(8,128)} %reduce-scatter.19.cloned.1.call-done) | data formatting | bytes 1179648
  693.0 12.2 %copy.70 = bf16[4,256,192]{1,0,2:T(4,128)(2,1)S(1)} copy(bf16[4,256,192]{0,2,1:T(8,128)(2,1)} %bitcast.123) | data formatting | bytes 786432
  705.3 29.3 %reshape.244 = bf16[256,192,4]{2,1,0:T(8,128)(2,1)} reshape(f32[256,768]{1,0:T(8,128)} %reduce-scatter.21.cloned.1.call-done) | data formatting | bytes 1179648
  734.6 12.2 %copy.72 = bf16[4,256,192]{1,0,2:T(4,128)(2,1)S(1)} copy(bf16[4,256,192]{0,2,1:T(8,128)(2,1)} %bitcast.124) | data formatting | bytes 786432
  749.3 2.9 copy.73
  752.2 2.9 reshape.245
  757.9 2.3 add_add_fusion
  760.4 5.8 fusion.34
  766.3 4.4 fusion.32
  774.1 3.9 copy.66
  778.1 15.8 %reduce-scatter.25.cloned.1.call-done = f32[96,192]{1,0:T(8,128)} async-done(((f32[768,192]{1,0:T(8,128)}), f32[96,192]{1,0:T(8,128)}) %reduce-scatter.25.cloned.1.call-update) | async-done | bytes 73744
  796.5 40.9 %reduce-scatter.23.cloned.1.call-done = f32[96,576]{1,0:T(8,128)} async-done(((f32[768,576]{1,0:T(8,128)}), f32[96,576]{1,0:T(8,128)}) %reduce-scatter.23.cloned.1.call-update) | async-done | bytes 221200
  839.3 121.4 %all-reduce.13.cloned.1.call-done = f32[1024,768]{1,0:T(8,128)} async-done(((f32[1024,768]{1,0:T(8,128)}), f32[1024,768]{1,0:T(8,128)}) %all-reduce.13.cloned.1.call-update) | async-done | bytes 3145744 | tf_op jit(solution)/shard_map/psum | solution.py:197
  960.8 3.0 multiply_reduce_fusion.1
  967.0 2.2 copy.67
  969.2 25.0 %all-reduce.1 = (f32[768]{0:T(1024)}, f32[2,192]{1,0:T(2,128)}, f32[768]{0:T(1024)}, f32[768]{0:T(1024)}, f32[768]{0:T(1024)}, /*index=5*/f32[768]{0:T(1024)}) all-reduce(f32[768]{0:T(1024)S(1)} %get-tuple-element.48, f32[2,192]{1,0:T(2,128)S(1)} %pad_maximum_fusion.2, ...), channel_id=1, replica_groups=mesh['shard'=2,'ctx'=4,'tp'=4] {'shard','ctx'}, use_global_device_ids=true, to_apply=%region_19.20 | all-reduce | flops 4224 | bytes 33792 | tf_op jit(solution)/shard_map/psum | solution.py:211
  994.2 11.9 %reduce-scatter.17.cloned.1.call-done = f32[768,96]{0,1:T(8,128)} async-done(((f32[768,768]{0,1:T(8,128)}), f32[768,96]{0,1:T(8,128)}) %reduce-scatter.17.cloned.1.call-update) | async-done | bytes 294928 | tf_op jit(solution)/shard_map/reduce_scatter | solution.py:209
  1006.1 46.2 %reduce-scatter.15.cloned.1.call-done = f32[96,768]{1,0:T(8,128)} async-done(((f32[768,768]{1,0:T(8,128)}), f32[96,768]{1,0:T(8,128)}) %reduce-scatter.15.cloned.1.call-update) | async-done | bytes 294928 | tf_op jit(solution)/shard_map/reduce_scatter | solution.py:208
  (233 shorter events, 60.3 us)
Async XLA Ops:
  8.0 6.5 copy-start.38
  8.0 48.6 %all-gather.7.cloned.1.call-start = ((), (), s32[]{:S(2)}) async-start(), calls=%async_computation.7 | async-start | bytes 1966080 | tf_op jit(solution)/shard_map/all_gather | solution.py:58
  13.3 198.3 %copy-start.1 = (f32[4,256,767]{2,1,0:T(8,128)}, f32[4,256,767]{2,1,0:T(8,128)S(1)}, u32[]{:S(2)}) copy-start(f32[4,256,767]{2,1,0:T(8,128)S(1)} %copy.52) | copy-start | bytes 9424900
  13.3 16.2 %copy-start.45 = (f32[768]{0:T(1024)S(1)}, f32[768]{0:T(1024)}, u32[]{:S(2)}) copy-start(f32[768]{0:T(1024)} %param.15) | copy-start | bytes 9220
  14.5 15.0 %copy-start.14 = (f32[1,1024]{0,1:T(8,128)S(1)}, f32[1,1024]{0,1:T(8,128)}, u32[]{:S(2)}) copy-start(f32[1,1024]{0,1:T(8,128)} %copy.81) | copy-start | bytes 12292
  33.0 43.2 %all-gather.5.cloned.1.call-start = ((), (), s32[]{:S(2)}) async-start(), calls=%async_computation.6 | async-start | bytes 1966080 | tf_op jit(solution)/shard_map/all_gather | solution.py:59
  33.1 21.4 %copy-start.59 = (s32[4]{0:T(128)S(1)}, s32[4]{0:T(128)}, u32[]{:S(2)}) copy-start(s32[4]{0:T(128)} %param.14) | copy-start | bytes 52
  36.3 173.0 %all-reduce.7.cloned.1.call-start = ((), (), s32[]{:S(2)}) async-start(), calls=%async_computation.8 | async-start | bytes 6291456 | tf_op jit(solution)/shard_map/psum | solution.py:90
  42.0 19.5 %copy-start.26 = (bf16[4,256,3,64]{1,0,3,2:T(4,128)(2,1)}, bf16[4,256,3,64]{1,0,3,2:T(4,128)(2,1)S(1)}, u32[]{:S(2)}) copy-start(bf16[4,256,3,64]{1,0,3,2:T(4,128)(2,1)S(1)} %reshape.226) | copy-start | bytes 1179652
  61.5 4.7 copy-start
  61.5 16.6 %copy-start.37 = (f32[4,3,256]{2,1,0:T(4,128)}, f32[4,3,256]{2,1,0:T(4,128)S(1)}, u32[]{:S(2)}) copy-start(f32[4,3,256]{2,1,0:T(4,128)S(1)} %get-tuple-element.72) | copy-start | bytes 36868
  78.1 6.6 copy-start.23
  78.1 7.7 copy-start.30
  88.1 127.8 %all-gather.9.cloned.1.call-start = ((), (), s32[]{:S(2)}) async-start(), calls=%async_computation.9 | async-start | bytes 1327104 | tf_op jit(solution)/shard_map/all_gather | solution.py:41
  88.7 132.7 %all-gather.11.cloned.1.call-start = ((), (), s32[]{:S(2)}) async-start(), calls=%async_computation.10 | async-start | bytes 1327104 | tf_op jit(solution)/shard_map/all_gather | solution.py:42
  89.3 262.2 %all-reduce.11.cloned.1.call-start = ((), (), s32[]{:S(2)}) async-start(), calls=%async_computation.12 | async-start | bytes 6291456 | tf_op jit(solution)/shard_map/psum | solution.py:128
  96.4 112.9 %copy-start.47 = (f32[768]{0:T(1024)S(1)}, f32[768]{0:T(1024)}, u32[]{:S(2)}) copy-start(f32[768]{0:T(1024)} %param.19) | copy-start | bytes 9220
  211.6 4.3 copy-start.48
  215.9 5.5 copy-start.42
  215.9 5.5 copy-start.36
  215.9 5.5 copy-start.63
  221.4 6.8 copy-start.62
  231.2 120.2 %copy-start.6 = (f32[1024,768]{1,0:T(8,128)S(1)}, f32[1024,768]{1,0:T(8,128)}, u32[]{:S(2)}) copy-start(f32[1024,768]{1,0:T(8,128)} %get-tuple-element.67) | copy-start | bytes 9437188
  231.3 432.5 %reduce-scatter.19.cloned.1.call-start = ((), (), s32[]{:S(2)}) async-start(), calls=%async_computation.16 | async-start | bytes 3932160
  351.5 3.8 copy-start.43
  361.6 9.5 slice-start
  361.6 9.5 slice-start.1
  363.4 7.6 slice-start.2
  509.3 196.1 %reduce-scatter.21.cloned.1.call-start = ((), (), s32[]{:S(2)}) async-start(), calls=%async_computation.17 | async-start | bytes 3932160
  648.7 6.4 copy-start.18
  648.7 6.4 copy-start.35
  648.7 122.0 %all-reduce.9.cloned.1.call-start = ((), (), s32[]{:S(2)}) async-start(), calls=%async_computation.11 | async-start | bytes 3145728 | tf_op jit(solution)/shard_map/psum | solution.py:101
  655.1 138.8 %reduce-scatter.25.cloned.1.call-start = ((), (), s32[]{:S(2)}) async-start(), calls=%async_computation.19 | async-start | bytes 884736
  656.8 6.5 copy-start.5
  656.8 180.6 %reduce-scatter.23.cloned.1.call-start = ((), (), s32[]{:S(2)}) async-start(), calls=%async_computation.18 | async-start | bytes 2211840
  705.3 41.6 %copy-start.32 = (bf16[24,8,4,256]{3,1,2,0:T(8,128)(2,1)}, bf16[24,8,4,256]{3,1,2,0:T(8,128)(2,1)S(1)}, u32[]{:S(2)}) copy-start(bf16[24,8,4,256]{3,1,2,0:T(8,128)(2,1)S(1)} %copy.85) | copy-start | bytes 1179652
  755.1 205.6 %all-reduce.13.cloned.1.call-start = ((), (), s32[]{:S(2)}) async-start(), calls=%async_computation.13 | async-start | bytes 6291456 | tf_op jit(solution)/shard_map/psum | solution.py:197
  760.3 6.0 copy-start.7
  760.3 6.0 copy-start.44
  760.3 6.0 copy-start.50
  760.3 245.8 %reduce-scatter.17.cloned.1.call-start = ((), (), s32[]{:S(2)}) async-start(), calls=%async_computation.15 | async-start | bytes 2654208 | tf_op jit(solution)/shard_map/reduce_scatter | solution.py:209
  766.2 4.6 copy-start.54
  766.2 286.1 %reduce-scatter.15.cloned.1.call-start = ((), (), s32[]{:S(2)}) async-start(), calls=%async_computation.14 | async-start | bytes 2654208 | tf_op jit(solution)/shard_map/reduce_scatter | solution.py:208
  772.6 22.9 %copy-start.29 = (bf16[4,256,192]{1,0,2:T(4,128)(2,1)S(1)}, bf16[4,256,192]{1,0,2:T(4,128)(2,1)}, u32[]{:S(2)}) copy-start(bf16[4,256,192]{1,0,2:T(4,128)(2,1)} %copy-done.28) | copy-start | bytes 1179652
  774.1 186.7 %copy-start.2 = (f32[4,256,767]{2,1,0:T(8,128)S(1)}, f32[4,256,767]{2,1,0:T(8,128)}, u32[]{:S(2)}) copy-start(f32[4,256,767]{2,1,0:T(8,128)} %copy-done.1) | copy-start | bytes 9424900
  774.1 186.7 %copy-start.41 = (f32[1024]{0:T(1024)S(1)}, f32[1024]{0:T(1024)}, u32[]{:S(2)}) copy-start(f32[1024]{0:T(1024)} %copy-done.40) | copy-start | bytes 12292
  774.1 186.7 %copy-start.46 = (f32[768]{0:T(1024)S(1)}, f32[768]{0:T(1024)}, u32[]{:S(2)}) copy-start(f32[768]{0:T(1024)} %param.15) | copy-start | bytes 9220
  960.8 4.1 copy-start.20
  (35 other events, 77.7 us)
Sparse Core Ops, SparseCore 0:
  33.1 21.6 all-gather.6
  56.4 19.7 all-gather.4
  88.2 121.0 all-reduce.6
  231.4 120.0 all-reduce.10
  509.4 36.8 reduce-scatter.18
  648.8 36.3 reduce-scatter.20
  687.6 68.9 all-reduce.8
  759.7 34.0 reduce-scatter.24
  797.3 40.1 reduce-scatter.22
  839.7 121.0 all-reduce.12
  964.7 41.4 reduce-scatter.16
  1009.9 42.3 reduce-scatter.14
Sparse Core Ops, SparseCore 1:
  90.5 23.8 all-gather.8
  116.1 23.8 all-gather.10
where the time goes:
time: 1070 us; the launch traced here: 1060 us
  waiting for transfers between devices  472 us (44%)
  local copies, waits for them, and re-layouts  400 us (37%)
  matrix products  69.9 us (7%)
  blocking collectives  50.5 us (5%)
  other arithmetic  48.4 us (5%)
  between operations  16.9 us (2%)
    unnamed x161, local copies, waits for them, and re-layouts  384 us
    psum x1, waiting for transfers between devices, shards(): first_grad = lax.psum(first_part, 'tp')  121 us
    psum x1, waiting for transfers between devices, shards(): second_grad = lax.psum(second_term, 'tp')  119 us
    psum x1, waiting for transfers between devices, shards(): branch = lax.psum(exit_term, 'tp') + exit_bias  109 us
    unnamed x18, waiting for transfers between devices  58 us
    reduce_scatter x1, waiting for transfers between devices, shards(): lax.psum_scatter(hidden_weight_grad, ('shard', 'ctx'), scatter_dimension=...  46.2 us
    psum x1, blocking collectives, shards(): lax.psum((first_gain_grad, entry_bias_grad, exit_bias_grad, second_gain_g...  25 us
  transfers between devices with their start and end apart: 14, of which 8 were waited for; matrix products, arithmetic and copies ran while one was open for 30% of the time, Pallas kernels for 0%

commit v1 on v0

--- a/solution.py
+++ b/solution.py
@@ -194,7 +194,7 @@
         + jnp.einsum("re,de->rd", key_low, full_entry[1], preferred_element_type=single)
         + jnp.einsum("re,de->rd", value_low, full_entry[2], preferred_element_type=single)
     )
-    first_grad = lax.psum(first_part, "tp")
+    first_grad = jnp.sum(lax.all_gather(first_part, "tp"), axis=0)
     first_gain_grad = jnp.sum(first_grad * first_unit, 0)
     first_scaled = first_grad * first_gain
     stream_grad = middle_grad + first_inverse * (

time: 1070 us -> 1160 us (1.084)
  waiting for transfers between devices: 472 us -> 560 us
    all_gather x0 -> x1, waiting for transfers between devices: none -> 218 us  [shards(): first_grad = jnp.sum(lax.all_gather(first_part, 'tp'), axis=0)]
    psum x1 -> x0, waiting for transfers between devices: 121 us -> none  [shards(): first_grad = lax.psum(first_part, 'tp')]
  transfers between devices with their start and end apart: 14 -> 14, of which waited for: 8 -> 8; matrix products, arithmetic and copies ran while one was open for 30% -> 28% of each run, Pallas kernels for 0% -> 0%
where the time goes in v1:
time: 1160 us
  waiting for transfers between devices  560 us (48%)
  local copies, waits for them, and re-layouts  400 us (34%)
  matrix products  69.8 us (6%)
  other arithmetic  56.2 us (5%)
  blocking collectives  50.8 us (4%)
  between operations  16.9 us (1%)
    unnamed x161, local copies, waits for them, and re-layouts  384 us
    all_gather x1, waiting for transfers between devices, shards(): first_grad = jnp.sum(lax.all_gather(first_part, 'tp'), axis=0)  218 us
    psum x1, waiting for transfers between devices, shards(): second_grad = lax.psum(second_term, 'tp')  119 us
    psum x1, waiting for transfers between devices, shards(): branch = lax.psum(exit_term, 'tp') + exit_bias  109 us
    unnamed x18, waiting for transfers between devices  58.3 us
    reduce_scatter x1, waiting for transfers between devices, shards(): lax.psum_scatter(hidden_weight_grad, ('shard', 'ctx'), scatter_dimension=...  46.1 us
    psum x1, blocking collectives, shards(): lax.psum((first_gain_grad, entry_bias_grad, exit_bias_grad, second_gain_g...  25.3 us
  transfers between devices with their start and end apart: 14, of which 8 were waited for; matrix products, arithmetic and copies ran while one was open for 28% of the time, Pallas kernels for 0%

profile of v1, /device:TPU:0, one launch (start us, length us, event | category | flops | bytes accessed | tf_op | source)
XLA Modules:
  0.0 1155.6 jit_solution(5058209637562011660)
XLA Ops:
  8.1 2.3 convert_reduce_fusion.5
  10.3 2.9 copy.52
  14.5 13.1 %all_gather.30 = bf16[3,768,192]{2,1,0:T(8,128)(2,1)S(1)} all-gather(bf16[3,96,192]{2,1,0:T(8,128)(2,1)S(1)} %copy-done.38), channel_id=1, replica_groups=mesh['shard'=2,'ctx'=4,'tp'=4] {'shard','ctx'}, dimensions={1}, use_global_device_ids=true | all-gather | bytes 995328 | tf_op jit(solution)/shard_map/all_gather | solution.py:39
  36.3 2.9 fusion.21
  42.1 12.4 %all_gather.33 = bf16[192,768]{0,1:T(8,128)(2,1)} all-gather(bf16[192,96]{0,1:T(8,128)(2,1)} %copy.58), channel_id=1, replica_groups=mesh['shard'=2,'ctx'=4,'tp'=4] {'shard','ctx'}, dimensions={1}, use_global_device_ids=true | all-gather | bytes 331776 | tf_op jit(solution)/shard_map/all_gather | solution.py:40
  58.6 2.9 fusion.38
  61.6 4.6 copy-done
  66.2 3.4 fusion.3
  69.6 6.6 all-gather.7.cloned.1.call-done
  78.1 6.6 fusion.24
  85.8 2.2 fusion.39
  89.6 4.3 copy.59
  99.9 109.4 %all-reduce.6.cloned.1.call-done = f32[1024,768]{1,0:T(8,128)} async-done(((f32[1024,768]{1,0:T(8,128)}), f32[1024,768]{1,0:T(8,128)}) %all-reduce.6.cloned.1.call-update) | async-done | bytes 3145744 | tf_op jit(solution)/shard_map/psum | solution.py:90
  209.3 2.2 add_reduce_fusion
  211.6 4.3 multiply_reduce_fusion.4
  215.9 5.5 fusion.33
  221.4 5.6 convert_reduce_fusion.1
  228.2 3.1 fusion.40
  232.5 119.0 %all-reduce.10.cloned.1.call-done = f32[1024,768]{1,0:T(8,128)} async-done(((f32[1024,768]{1,0:T(8,128)}), f32[1024,768]{1,0:T(8,128)}) %all-reduce.10.cloned.1.call-update) | async-done | bytes 3145744 | tf_op jit(solution)/shard_map/psum | solution.py:128
  351.5 3.5 multiply_reduce_fusion
  363.4 7.6 fusion
  371.1 3.0 fusion.2
  376.7 48.2 %copy.69 = f32[4,1024,192]{0,2,1:T(8,128)} copy(f32[4,1024,192]{1,2,0:T(8,128)S(1)} %bitcast.134) | data formatting | bytes 6291456
  424.9 84.3 %reshape.242 = f32[1024,768]{1,0:T(8,128)} reshape(f32[1024,192,4]{2,1,0:T(8,128)} %bitcast.23) | data formatting | bytes 6291456
  509.8 6.3 fusion.5
  516.1 48.3 %copy.71 = f32[4,1024,192]{0,2,1:T(8,128)} copy(f32[4,1024,192]{1,2,0:T(8,128)S(1)} %bitcast.128) | data formatting | bytes 6291456
  564.3 84.3 %reshape.244 = f32[1024,768]{1,0:T(8,128)} reshape(f32[1024,192,4]{2,1,0:T(8,128)} %bitcast.26) | data formatting | bytes 6291456
  649.9 5.1 convolution_convert_fusion.1
  657.0 5.1 convert_reduce_fusion.4
  663.8 29.2 %reshape.243 = bf16[256,192,4]{2,1,0:T(8,128)(2,1)} reshape(f32[256,768]{1,0:T(8,128)} %reduce-scatter.19.cloned.1.call-done) | data formatting | bytes 1179648
  693.0 12.2 %copy.70 = bf16[4,256,192]{1,0,2:T(4,128)(2,1)S(1)} copy(bf16[4,256,192]{0,2,1:T(8,128)(2,1)} %bitcast.124) | data formatting | bytes 786432
  705.3 29.3 %reshape.245 = bf16[256,192,4]{2,1,0:T(8,128)(2,1)} reshape(f32[256,768]{1,0:T(8,128)} %reduce-scatter.21.cloned.1.call-done) | data formatting | bytes 1179648
  734.6 12.2 %copy.72 = bf16[4,256,192]{1,0,2:T(4,128)(2,1)S(1)} copy(bf16[4,256,192]{0,2,1:T(8,128)(2,1)} %bitcast.125) | data formatting | bytes 786432
  749.3 2.9 copy.73
  752.2 2.8 reshape.246
  757.9 2.3 add_add_fusion
  760.3 5.8 fusion.34
  766.2 4.4 fusion.32
  773.9 3.8 copy.66
  777.8 16.0 %reduce-scatter.25.cloned.1.call-done = f32[96,192]{1,0:T(8,128)} async-done(((f32[768,192]{1,0:T(8,128)}), f32[96,192]{1,0:T(8,128)}) %reduce-scatter.25.cloned.1.call-update) | async-done | bytes 73744
  796.5 40.9 %reduce-scatter.23.cloned.1.call-done = f32[96,576]{1,0:T(8,128)} async-done(((f32[768,576]{1,0:T(8,128)}), f32[96,576]{1,0:T(8,128)}) %reduce-scatter.23.cloned.1.call-update) | async-done | bytes 221200
  839.4 217.7 %all-gather.15.cloned.1.call-done = f32[4096,768]{1,0:T(8,128)} async-done(((f32[1024,768]{1,0:T(8,128)}), f32[4096,768]{1,0:T(8,128)}) %all-gather.15.cloned.1.call-update) | async-done | bytes 12582928 | tf_op jit(solution)/shard_map/all_gather | solution.py:197
  1057.1 7.6 reduce_sum.181
  1064.7 3.2 multiply_reduce_fusion.1
  1071.4 2.2 copy.67
  1073.6 25.3 %all-reduce.1 = (f32[768]{0:T(1024)}, f32[2,192]{1,0:T(2,128)}, f32[768]{0:T(1024)}, f32[768]{0:T(1024)}, f32[768]{0:T(1024)}, /*index=5*/f32[768]{0:T(1024)}) all-reduce(f32[768]{0:T(1024)S(1)} %get-tuple-element.48, f32[2,192]{1,0:T(2,128)S(1)} %pad_maximum_fusion.2, ...), channel_id=1, replica_groups=mesh['shard'=2,'ctx'=4,'tp'=4] {'shard','ctx'}, use_global_device_ids=true, to_apply=%region_19.20 | all-reduce | flops 4224 | bytes 33792 | tf_op jit(solution)/shard_map/psum | solution.py:211
  1098.9 2.9 reduce-scatter.17.cloned.1.call-done
  1101.8 46.1 %reduce-scatter.15.cloned.1.call-done = f32[96,768]{1,0:T(8,128)} async-done(((f32[768,768]{1,0:T(8,128)}), f32[96,768]{1,0:T(8,128)}) %reduce-scatter.15.cloned.1.call-update) | async-done | bytes 294928 | tf_op jit(solution)/shard_map/reduce_scatter | solution.py:208
  (234 shorter events, 62.8 us)
Async XLA Ops:
  8.0 6.5 copy-start.38
  8.0 48.6 %all-gather.9.cloned.1.call-start = ((), (), s32[]{:S(2)}) async-start(), calls=%async_computation.7 | async-start | bytes 1966080 | tf_op jit(solution)/shard_map/all_gather | solution.py:58
  13.3 198.3 %copy-start.1 = (f32[4,256,767]{2,1,0:T(8,128)}, f32[4,256,767]{2,1,0:T(8,128)S(1)}, u32[]{:S(2)}) copy-start(f32[4,256,767]{2,1,0:T(8,128)S(1)} %copy.52) | copy-start | bytes 9424900
  13.3 16.2 %copy-start.45 = (f32[768]{0:T(1024)S(1)}, f32[768]{0:T(1024)}, u32[]{:S(2)}) copy-start(f32[768]{0:T(1024)} %param.15) | copy-start | bytes 9220
  14.5 15.0 %copy-start.15 = (f32[1,1024]{0,1:T(8,128)S(1)}, f32[1,1024]{0,1:T(8,128)}, u32[]{:S(2)}) copy-start(f32[1,1024]{0,1:T(8,128)} %copy.81) | copy-start | bytes 12292
  33.0 43.2 %all-gather.7.cloned.1.call-start = ((), (), s32[]{:S(2)}) async-start(), calls=%async_computation.6 | async-start | bytes 1966080 | tf_op jit(solution)/shard_map/all_gather | solution.py:59
  33.1 21.4 %copy-start.59 = (s32[4]{0:T(128)S(1)}, s32[4]{0:T(128)}, u32[]{:S(2)}) copy-start(s32[4]{0:T(128)} %param.14) | copy-start | bytes 52
  36.3 173.0 %all-reduce.6.cloned.1.call-start = ((), (), s32[]{:S(2)}) async-start(), calls=%async_computation.8 | async-start | bytes 6291456 | tf_op jit(solution)/shard_map/psum | solution.py:90
  42.0 19.5 %copy-start.26 = (bf16[4,256,3,64]{1,0,3,2:T(4,128)(2,1)}, bf16[4,256,3,64]{1,0,3,2:T(4,128)(2,1)S(1)}, u32[]{:S(2)}) copy-start(bf16[4,256,3,64]{1,0,3,2:T(4,128)(2,1)S(1)} %reshape.226) | copy-start | bytes 1179652
  61.5 4.7 copy-start
  61.5 16.6 %copy-start.37 = (f32[4,3,256]{2,1,0:T(4,128)}, f32[4,3,256]{2,1,0:T(4,128)S(1)}, u32[]{:S(2)}) copy-start(f32[4,3,256]{2,1,0:T(4,128)S(1)} %get-tuple-element.72) | copy-start | bytes 36868
  78.1 6.6 copy-start.23
  78.1 7.7 copy-start.30
  88.1 127.8 %all-gather.11.cloned.1.call-start = ((), (), s32[]{:S(2)}) async-start(), calls=%async_computation.9 | async-start | bytes 1327104 | tf_op jit(solution)/shard_map/all_gather | solution.py:41
  88.7 132.7 %all-gather.13.cloned.1.call-start = ((), (), s32[]{:S(2)}) async-start(), calls=%async_computation.10 | async-start | bytes 1327104 | tf_op jit(solution)/shard_map/all_gather | solution.py:42
  89.3 262.2 %all-reduce.10.cloned.1.call-start = ((), (), s32[]{:S(2)}) async-start(), calls=%async_computation.12 | async-start | bytes 6291456 | tf_op jit(solution)/shard_map/psum | solution.py:128
  96.4 112.9 %copy-start.47 = (f32[768]{0:T(1024)S(1)}, f32[768]{0:T(1024)}, u32[]{:S(2)}) copy-start(f32[768]{0:T(1024)} %param.19) | copy-start | bytes 9220
  211.6 4.3 copy-start.48
  215.9 5.5 copy-start.42
  215.9 5.5 copy-start.36
  215.9 5.5 copy-start.63
  221.4 6.8 copy-start.62
  231.2 120.2 %copy-start.6 = (f32[1024,768]{1,0:T(8,128)S(1)}, f32[1024,768]{1,0:T(8,128)}, u32[]{:S(2)}) copy-start(f32[1024,768]{1,0:T(8,128)} %get-tuple-element.67) | copy-start | bytes 9437188
  231.3 432.5 %reduce-scatter.19.cloned.1.call-start = ((), (), s32[]{:S(2)}) async-start(), calls=%async_computation.16 | async-start | bytes 3932160
  361.6 9.5 slice-start
  361.6 9.5 slice-start.1
  363.4 7.6 slice-start.2
  509.3 196.1 %reduce-scatter.21.cloned.1.call-start = ((), (), s32[]{:S(2)}) async-start(), calls=%async_computation.17 | async-start | bytes 3932160
  648.7 6.5 copy-start.19
  648.7 6.5 copy-start.35
  648.7 121.9 %all-reduce.8.cloned.1.call-start = ((), (), s32[]{:S(2)}) async-start(), calls=%async_computation.11 | async-start | bytes 3145728 | tf_op jit(solution)/shard_map/psum | solution.py:101
  655.1 138.8 %reduce-scatter.25.cloned.1.call-start = ((), (), s32[]{:S(2)}) async-start(), calls=%async_computation.19 | async-start | bytes 884736
  656.8 6.5 copy-start.5
  656.8 180.7 %reduce-scatter.23.cloned.1.call-start = ((), (), s32[]{:S(2)}) async-start(), calls=%async_computation.18 | async-start | bytes 2211840
  705.3 41.6 %copy-start.32 = (bf16[24,8,4,256]{3,1,2,0:T(8,128)(2,1)}, bf16[24,8,4,256]{3,1,2,0:T(8,128)(2,1)S(1)}, u32[]{:S(2)}) copy-start(bf16[24,8,4,256]{3,1,2,0:T(8,128)(2,1)S(1)} %copy.85) | copy-start | bytes 1179652
  755.1 302.0 %all-gather.15.cloned.1.call-start = ((), (), s32[]{:S(2)}) async-start(), calls=%async_computation.15 | async-start | bytes 15728640 | tf_op jit(solution)/shard_map/all_gather | solution.py:197
  760.2 5.9 copy-start.7
  760.2 5.9 copy-start.44
  760.2 5.9 copy-start.50
  760.3 341.5 %reduce-scatter.17.cloned.1.call-start = ((), (), s32[]{:S(2)}) async-start(), calls=%async_computation.14 | async-start | bytes 2654208 | tf_op jit(solution)/shard_map/reduce_scatter | solution.py:209
  766.1 4.5 copy-start.54
  766.1 381.8 %reduce-scatter.15.cloned.1.call-start = ((), (), s32[]{:S(2)}) async-start(), calls=%async_computation.13 | async-start | bytes 2654208 | tf_op jit(solution)/shard_map/reduce_scatter | solution.py:208
  773.9 21.6 %copy-start.29 = (bf16[4,256,192]{1,0,2:T(4,128)(2,1)S(1)}, bf16[4,256,192]{1,0,2:T(4,128)(2,1)}, u32[]{:S(2)}) copy-start(bf16[4,256,192]{1,0,2:T(4,128)(2,1)} %copy-done.28) | copy-start | bytes 1179652
  1057.1 7.6 copy-start.2
  1057.1 7.6 copy-start.41
  1057.1 7.6 copy-start.46
  1064.7 4.5 copy-start.12
  1064.7 4.5 copy-start.17
  (35 other events, 78.7 us)
Sparse Core Ops, SparseCore 0:
  33.1 21.6 all-gather.8
  56.4 19.7 all-gather.6
  88.2 121.0 all-reduce.5
  231.4 120.0 all-reduce.9
  509.4 36.8 reduce-scatter.18
  648.8 36.3 reduce-scatter.20
  687.6 68.9 all-reduce.7
  759.7 34.0 reduce-scatter.24
  797.3 40.1 reduce-scatter.22
  838.9 218.1 all-gather.14
  1061.0 40.7 reduce-scatter.16
  1105.6 42.3 reduce-scatter.14
Sparse Core Ops, SparseCore 1:
  90.5 23.8 all-gather.10
  116.1 23.8 all-gather.12
